TPU v7x, 32 devices: a whole 2x2x4 slice. The times are simulated.
32 devices in a mesh: groups: 2 (over x), azim: 16 (over z, y, core).
Axes of the slice: x: 2, y: 2, z: 4, core: 2. Of those that a mesh axis runs over, the one named last changes fastest.
Arguments:
- conserved: float32 [5, 256, 2048], P(None, ('groups', 'azim')), parts along dimension 1, may hold values from -6 to 6
- velocity: float32 [256, 2048], P(('groups', 'azim')), parts along dimension 0, may hold values from -0.8 to 0.8
- viscosity: float32 [5], replicated, may hold values from 0.02 to 0.1
- shifts: int32 [4, 64], P('groups'), parts along dimension 0, may hold values from 0 to 127
Outputs:
- advanced: float32 [5, 256, 2048], P(None, ('groups', 'azim')), parts along dimension 1
There are 2 independent parts, one for each index of `groups`. A program takes and returns all parts, laid end to end along the dimension named above; an argument that names none is the same for every part. Nothing has to cross between parts.
All inputs are finite; a program needn't handle non-finite values.
Results may differ from a plain program's by a relative error of at most 0.0003.
Values sent between devices are 32-bit elements; how exact they have to be, the bound alone decides.
A program may use at most 64 MiB of HBM per device.

v0:
```python
import jax
import jax.numpy as jnp
from jax import lax
from jax.sharding import PartitionSpec as P

STEPS = 2


def padded(cells, sides, width):
    for axis, dim in sides:
        count = lax.axis_size(axis)
        head = lax.slice_in_dim(cells, 0, width, axis=dim)
        tail = lax.slice_in_dim(cells, cells.shape[dim] - width, cells.shape[dim], axis=dim)
        cells = jnp.concatenate(
            [
                lax.ppermute(tail, axis, [(i, (i + 1) % count) for i in range(count)]),
                cells,
                lax.ppermute(head, axis, [((i + 1) % count, i) for i in range(count)]),
            ],
            axis=dim,
        )
    return cells


def shifted(value, axis, steps):
    count = lax.axis_size(axis)
    pairs = [(source, (source + steps) % count) for source in range(count)]
    return lax.ppermute(value, axis, pairs)


def minmod(left, right):
    return 0.5 * (jnp.sign(left) + jnp.sign(right)) * jnp.minimum(jnp.abs(left), jnp.abs(right))


def lateral_sum(inner, heights):
    width = inner.shape[2]
    height_of = jnp.arange(width, dtype=jnp.int32) % heights
    outward = jnp.concatenate([inner[:, :, heights:], inner[:, :, width - heights :]], axis=2)
    inward = jnp.concatenate([inner[:, :, :heights], inner[:, :, : width - heights]], axis=2)
    upper = jnp.concatenate([inner[:, :, 1:], inner[:, :, width - 1 :]], axis=2)
    upper = jnp.where((height_of == heights - 1)[None, None, :], inner, upper)
    lower = jnp.concatenate([inner[:, :, :1], inner[:, :, : width - 1]], axis=2)
    lower = jnp.where((height_of == 0)[None, None, :], inner, lower)
    return outward + inward + upper + lower - 4.0 * inner


def tendency(ext, speed, viscosity, heights):
    count = ext.shape[1]
    diff = ext[:, 1:] - ext[:, :-1]
    slope = minmod(diff[:, :-1], diff[:, 1:])
    left_state = ext[:, 1 : count - 2] + 0.5 * slope[:, 0 : count - 3]
    right_state = ext[:, 2 : count - 1] - 0.5 * slope[:, 1 : count - 2]
    face_speed = 0.5 * (speed[1 : count - 2] + speed[2 : count - 1])
    flux = jnp.maximum(face_speed, 0.0) * left_state + jnp.minimum(face_speed, 0.0) * right_state
    inner = ext[:, 2 : count - 2]
    azimuthal = ext[:, 3 : count - 1] + ext[:, 1 : count - 3] - 2.0 * inner
    lateral = lateral_sum(inner, heights)
    return -(flux[:, 1:] - flux[:, :-1]) + viscosity[:, None, None] * (azimuthal + lateral)


def section_rim(field):
    return padded(field, (("azim", 1),), 2)


def slide_down(joined, amount, limit):
    current = joined
    level = 0
    while 1 << level < limit:
        stride = 1 << level
        taken = amount >> level & 1 == 1
        moved = jnp.concatenate(
            [jnp.zeros_like(current[:, :stride]), current[:, : current.shape[1] - stride]], axis=1
        )
        current = jnp.where(taken[None, None, :], moved, current)
        level = level + 1
    return current


def local(conserved, velocity, viscosity, shifts):
    state = conserved
    block = state.shape[1]
    heights = state.shape[2] // shifts.shape[1]
    devices = lax.axis_size("azim")
    levels = devices.bit_length() - 1
    speed_wide = padded(velocity, (("azim", 0),), 6)
    speed_near = speed_wide[4:-4]
    for step in range(STEPS):
        first = state + tendency(section_rim(state), speed_near, viscosity, heights)
        second = 0.75 * state + 0.25 * (
            first + tendency(section_rim(first), speed_near, viscosity, heights)
        )
        third = 1.0 / 3.0 * state + 2.0 / 3.0 * (
            second + tendency(section_rim(second), speed_near, viscosity, heights)
        )
        per_column = jnp.repeat(shifts[step], heights)
        whole_blocks = per_column // block
        remainder = per_column - whole_blocks * block
        moved = third
        for level in range(levels):
            taken = whole_blocks >> level & 1 == 1
            arrived = shifted(moved, "azim", 1 << level)
            moved = jnp.where(taken[None, None, :], arrived, moved)
        preceding = shifted(moved, "azim", 1)
        joined = jnp.concatenate([preceding, moved], axis=1)
        state = slide_down(joined, remainder, block)[:, block:]
    return state


def solution(mesh):
    in_specs = (
        P(None, ("groups", "azim"), None),
        P(("groups", "azim"), None),
        P(),
        P("groups", None),
    )
    out_specs = P(None, ("groups", "azim"), None)
    return jax.shard_map(local, mesh=mesh, in_specs=in_specs, out_specs=out_specs, check_vma=False)
```

profile of v0, /device:TPU:0, one launch (start us, length us, event | category | flops | bytes accessed | tf_op | source)
XLA Modules:
  0.0 163.5 jit_solution(2882082080049075798)
XLA Ops:
  0.0 0.9 fusion.143
  0.9 0.5 collective-permute-start
  1.4 5.1 %collective-permute-start.1 = (f32[6,2048]{1,0:T(8,128)S(1)}, f32[6,2048]{1,0:T(8,128)S(1)}, u32[]{:S(2)}, u32[]{:S(2)}) collective-permute-start(f32[6,2048]{1,0:T(8,128)S(1)} %get-tuple-element.68), channel_id=1, source_target_pairs={{1,0},{2,1},{3,2},{4,3},{5,4},{6,5},{7,6},{8,7},{9,8},{10,9},{11,1... | collective-permute-start | bytes 147464 | tf_op jit(solution)/shard_map/ppermute | solution.py:18
  6.5 1.1 fusion.142
  7.7 4.4 %collective-permute-start.3 = (f32[5,2,2048]{2,1,0:T(2,128)S(1)}, f32[5,2,2048]{2,1,0:T(2,128)S(1)}, u32[]{:S(2)}, u32[]{:S(2)}) collective-permute-start(f32[5,2,2048]{2,1,0:T(2,128)S(1)} %get-tuple-element.63), channel_id=1, source_target_pairs={{1,0},{2,1},{3,2},{4,3},{5,4},{6,5},{7,6},{8,7},{9,8},{10,9},{11,1... | collective-permute-start | bytes 245768 | tf_op jit(solution)/shard_map/ppermute | solution.py:18
  12.2 0.2 fusion.139
  12.3 0.2 fusion.141
  12.7 0.7 copy-done.1
  13.4 0.9 collective-permute-done.2
  14.3 0.1 pad_maximum_fusion.2
  14.5 0.5 minimum_multiply_fusion.5
  15.0 0.3 fusion.31
  15.3 0.6 copy-done.2
  15.9 0.4 fusion.82
  16.4 0.2 fusion.134
  16.6 0.2 fusion.136
  16.8 4.5 %collective-permute-start.5 = (f32[5,2,2048]{2,1,0:T(2,128)S(1)}, f32[5,2,2048]{2,1,0:T(2,128)S(1)}, u32[]{:S(2)}, u32[]{:S(2)}) collective-permute-start(f32[5,2,2048]{2,1,0:T(2,128)S(1)} %get-tuple-element.53), channel_id=1, source_target_pairs={{1,0},{2,1},{3,2},{4,3},{5,4},{6,5},{7,6},{8,7},{9,8},{10,9},{11,1... | collective-permute-start | bytes 245768 | tf_op jit(solution)/shard_map/ppermute | solution.py:18
  21.4 2.0 %collective-permute-done.4 = f32[5,2,2048]{2,1,0:T(2,128)S(1)} collective-permute-done((f32[5,2,2048]{2,1,0:T(2,128)S(1)}, f32[5,2,2048]{2,1,0:T(2,128)S(1)}, u32[]{:S(2)}, u32[]{:S(2)}) %collective-permute-start.4) | collective-permute-done | bytes 81952 | tf_op jit(solution)/shard_map/ppermute | solution.py:16
  23.4 0.1 pad_maximum_fusion.3
  23.6 0.5 minimum_multiply_fusion.4
  24.0 0.3 fusion.26
  24.3 0.5 fusion.75
  24.9 0.2 fusion.129
  25.0 0.2 fusion.131
  25.3 4.5 %collective-permute-start.7 = (f32[5,2,2048]{2,1,0:T(2,128)S(1)}, f32[5,2,2048]{2,1,0:T(2,128)S(1)}, u32[]{:S(2)}, u32[]{:S(2)}) collective-permute-start(f32[5,2,2048]{2,1,0:T(2,128)S(1)} %get-tuple-element.43), channel_id=1, source_target_pairs={{1,0},{2,1},{3,2},{4,3},{5,4},{6,5},{7,6},{8,7},{9,8},{10,9},{11,1... | collective-permute-start | bytes 245768 | tf_op jit(solution)/shard_map/ppermute | solution.py:18
  29.9 2.0 %collective-permute-done.6 = f32[5,2,2048]{2,1,0:T(2,128)S(1)} collective-permute-done((f32[5,2,2048]{2,1,0:T(2,128)S(1)}, f32[5,2,2048]{2,1,0:T(2,128)S(1)}, u32[]{:S(2)}, u32[]{:S(2)}) %collective-permute-start.6) | collective-permute-done | bytes 81952 | tf_op jit(solution)/shard_map/ppermute | solution.py:16
  31.9 0.1 pad_maximum_fusion.4
  32.1 0.5 minimum_multiply_fusion.3
  32.6 0.3 fusion.21
  32.9 0.5 fusion.66
  33.4 0.1 copy-done.3
  33.7 8.9 %collective-permute-done.8 = f32[5,8,2048]{2,1,0:T(8,128)S(1)} collective-permute-done((f32[5,8,2048]{2,1,0:T(8,128)S(1)}, f32[5,8,2048]{2,1,0:T(8,128)S(1)}, u32[]{:S(2)}, u32[]{:S(2)}) %collective-permute-start.8) | collective-permute-done | bytes 327712 | tf_op jit(solution)/shard_map/ppermute | solution.py:28
  42.8 10.3 %collective-permute-done.9 = f32[5,8,2048]{2,1,0:T(8,128)S(1)} collective-permute-done((f32[5,8,2048]{2,1,0:T(8,128)S(1)}, f32[5,8,2048]{2,1,0:T(8,128)S(1)}, u32[]{:S(2)}, u32[]{:S(2)}) %collective-permute-start.9) | collective-permute-done | bytes 327712 | tf_op jit(solution)/shard_map/ppermute | solution.py:28
  53.2 11.7 %collective-permute-done.10 = f32[5,8,2048]{2,1,0:T(8,128)S(1)} collective-permute-done((f32[5,8,2048]{2,1,0:T(8,128)S(1)}, f32[5,8,2048]{2,1,0:T(8,128)S(1)}, u32[]{:S(2)}, u32[]{:S(2)}) %collective-permute-start.10) | collective-permute-done | bytes 327712 | tf_op jit(solution)/shard_map/ppermute | solution.py:28
  65.0 10.5 %collective-permute-done.11 = f32[5,8,2048]{2,1,0:T(8,128)S(1)} collective-permute-done((f32[5,8,2048]{2,1,0:T(8,128)S(1)}, f32[5,8,2048]{2,1,0:T(8,128)S(1)}, u32[]{:S(2)}, u32[]{:S(2)}) %collective-permute-start.11) | collective-permute-done | bytes 327712 | tf_op jit(solution)/shard_map/ppermute | solution.py:28
  75.7 9.2 %collective-permute-done.12 = f32[5,8,2048]{2,1,0:T(8,128)S(1)} collective-permute-done((f32[5,8,2048]{2,1,0:T(8,128)S(1)}, f32[5,8,2048]{2,1,0:T(8,128)S(1)}, u32[]{:S(2)}, u32[]{:S(2)}) %collective-permute-start.12) | collective-permute-done | bytes 327712 | tf_op jit(solution)/shard_map/ppermute | solution.py:28
  85.3 0.2 fusion.116
  85.4 0.2 fusion.114
  85.7 4.4 %collective-permute-start.14 = (f32[5,2,2048]{2,1,0:T(2,128)S(1)}, f32[5,2,2048]{2,1,0:T(2,128)S(1)}, u32[]{:S(2)}, u32[]{:S(2)}) collective-permute-start(f32[5,2,2048]{2,1,0:T(2,128)S(1)} %get-tuple-element.13), channel_id=1, source_target_pairs={{1,0},{2,1},{3,2},{4,3},{5,4},{6,5},{7,6},{8,7},{9,8},{10,9},{11,1... | collective-permute-start | bytes 245768 | tf_op jit(solution)/shard_map/ppermute | solution.py:18
  90.2 2.0 %collective-permute-done.13 = f32[5,2,2048]{2,1,0:T(2,128)S(1)} collective-permute-done((f32[5,2,2048]{2,1,0:T(2,128)S(1)}, f32[5,2,2048]{2,1,0:T(2,128)S(1)}, u32[]{:S(2)}, u32[]{:S(2)}) %collective-permute-start.13) | collective-permute-done | bytes 81952 | tf_op jit(solution)/shard_map/ppermute | solution.py:16
  92.4 0.5 minimum_multiply_fusion.2
  92.9 0.3 fusion.16
  93.2 0.4 fusion.57
  93.7 0.2 fusion.124
  93.9 0.2 fusion.126
  94.1 4.6 %collective-permute-start.16 = (f32[5,2,2048]{2,1,0:T(2,128)S(1)}, f32[5,2,2048]{2,1,0:T(2,128)S(1)}, u32[]{:S(2)}, u32[]{:S(2)}) collective-permute-start(f32[5,2,2048]{2,1,0:T(2,128)S(1)} %get-tuple-element.33), channel_id=1, source_target_pairs={{1,0},{2,1},{3,2},{4,3},{5,4},{6,5},{7,6},{8,7},{9,8},{10,9},{11,1... | collective-permute-start | bytes 245768 | tf_op jit(solution)/shard_map/ppermute | solution.py:18
  98.8 2.0 %collective-permute-done.15 = f32[5,2,2048]{2,1,0:T(2,128)S(1)} collective-permute-done((f32[5,2,2048]{2,1,0:T(2,128)S(1)}, f32[5,2,2048]{2,1,0:T(2,128)S(1)}, u32[]{:S(2)}, u32[]{:S(2)}) %collective-permute-start.15) | collective-permute-done | bytes 81952 | tf_op jit(solution)/shard_map/ppermute | solution.py:16
  101.0 0.5 minimum_multiply_fusion.1
  101.4 0.3 fusion.11
  101.7 0.5 fusion.50
  102.3 0.2 fusion.119
  102.4 0.2 fusion.121
  102.7 4.7 %collective-permute-start.18 = (f32[5,2,2048]{2,1,0:T(2,128)S(1)}, f32[5,2,2048]{2,1,0:T(2,128)S(1)}, u32[]{:S(2)}, u32[]{:S(2)}) collective-permute-start(f32[5,2,2048]{2,1,0:T(2,128)S(1)} %get-tuple-element.23), channel_id=1, source_target_pairs={{1,0},{2,1},{3,2},{4,3},{5,4},{6,5},{7,6},{8,7},{9,8},{10,9},{11,1... | collective-permute-start | bytes 245768 | tf_op jit(solution)/shard_map/ppermute | solution.py:18
  107.5 1.8 %collective-permute-done.17 = f32[5,2,2048]{2,1,0:T(2,128)S(1)} collective-permute-done((f32[5,2,2048]{2,1,0:T(2,128)S(1)}, f32[5,2,2048]{2,1,0:T(2,128)S(1)}, u32[]{:S(2)}, u32[]{:S(2)}) %collective-permute-start.17) | collective-permute-done | bytes 81952 | tf_op jit(solution)/shard_map/ppermute | solution.py:16
  109.3 0.2 collective-permute-done.18
  109.7 0.5 minimum_multiply_fusion
  110.1 0.3 fusion.6
  110.4 0.5 fusion.41
  111.2 9.1 %collective-permute-done.19 = f32[5,8,2048]{2,1,0:T(8,128)S(1)} collective-permute-done((f32[5,8,2048]{2,1,0:T(8,128)S(1)}, f32[5,8,2048]{2,1,0:T(8,128)S(1)}, u32[]{:S(2)}, u32[]{:S(2)}) %collective-permute-start.19) | collective-permute-done | bytes 327712 | tf_op jit(solution)/shard_map/ppermute | solution.py:28
  120.4 10.3 %collective-permute-done.20 = f32[5,8,2048]{2,1,0:T(8,128)S(1)} collective-permute-done((f32[5,8,2048]{2,1,0:T(8,128)S(1)}, f32[5,8,2048]{2,1,0:T(8,128)S(1)}, u32[]{:S(2)}, u32[]{:S(2)}) %collective-permute-start.20) | collective-permute-done | bytes 327712 | tf_op jit(solution)/shard_map/ppermute | solution.py:28
  130.8 11.8 %collective-permute-done.21 = f32[5,8,2048]{2,1,0:T(8,128)S(1)} collective-permute-done((f32[5,8,2048]{2,1,0:T(8,128)S(1)}, f32[5,8,2048]{2,1,0:T(8,128)S(1)}, u32[]{:S(2)}, u32[]{:S(2)}) %collective-permute-start.21) | collective-permute-done | bytes 327712 | tf_op jit(solution)/shard_map/ppermute | solution.py:28
  142.7 10.5 %collective-permute-done.22 = f32[5,8,2048]{2,1,0:T(8,128)S(1)} collective-permute-done((f32[5,8,2048]{2,1,0:T(8,128)S(1)}, f32[5,8,2048]{2,1,0:T(8,128)S(1)}, u32[]{:S(2)}, u32[]{:S(2)}) %collective-permute-start.22) | collective-permute-done | bytes 327712 | tf_op jit(solution)/shard_map/ppermute | solution.py:28
  153.3 9.2 %collective-permute-done.23 = f32[5,8,2048]{2,1,0:T(8,128)S(1)} collective-permute-done((f32[5,8,2048]{2,1,0:T(8,128)S(1)}, f32[5,8,2048]{2,1,0:T(8,128)S(1)}, u32[]{:S(2)}, u32[]{:S(2)}) %collective-permute-start.23) | collective-permute-done | bytes 327712 | tf_op jit(solution)/shard_map/ppermute | solution.py:28
  162.7 0.8 slice_select_fusion
  (81 shorter events, 3.9 us)
Async XLA Ops:
  0.0 12.1 %copy-start = (f32[5,8,2048]{2,1,0:T(8,128)S(1)}, f32[5,8,2048]{2,1,0:T(8,128)}, u32[]{:S(2)}) copy-start(f32[5,8,2048]{2,1,0:T(8,128)} %param.4) | copy-start | bytes 983044
  0.9 11.7 %collective-permute-start = (f32[6,2048]{1,0:T(8,128)S(1)}, f32[6,2048]{1,0:T(8,128)S(1)}, u32[]{:S(2)}, u32[]{:S(2)}) collective-permute-start(f32[6,2048]{1,0:T(8,128)S(1)} %get-tuple-element.67), channel_id=1, source_target_pairs={{0,1},{1,2},{2,3},{3,4},{4,5},{5,6},{6,7},{7,8},{8,9},{9,10},{10,1... | collective-permute-start | bytes 147464 | tf_op jit(solution)/shard_map/ppermute | solution.py:16
  1.4 11.2 %collective-permute-start.1 = (f32[6,2048]{1,0:T(8,128)S(1)}, f32[6,2048]{1,0:T(8,128)S(1)}, u32[]{:S(2)}, u32[]{:S(2)}) collective-permute-start(f32[6,2048]{1,0:T(8,128)S(1)} %get-tuple-element.68), channel_id=1, source_target_pairs={{1,0},{2,1},{3,2},{4,3},{5,4},{6,5},{7,6},{8,7},{9,8},{10,9},{11,1... | collective-permute-start | bytes 147464 | tf_op jit(solution)/shard_map/ppermute | solution.py:18
  7.6 6.6 %collective-permute-start.2 = (f32[5,2,2048]{2,1,0:T(2,128)S(1)}, f32[5,2,2048]{2,1,0:T(2,128)S(1)}, u32[]{:S(2)}, u32[]{:S(2)}) collective-permute-start(f32[5,2,2048]{2,1,0:T(2,128)S(1)} %get-tuple-element.64), channel_id=1, source_target_pairs={{0,1},{1,2},{2,3},{3,4},{4,5},{5,6},{6,7},{7,8},{8,9},{9,10},{10,1... | collective-permute-start | bytes 245768 | tf_op jit(solution)/shard_map/ppermute | solution.py:16
  7.7 6.6 %collective-permute-start.3 = (f32[5,2,2048]{2,1,0:T(2,128)S(1)}, f32[5,2,2048]{2,1,0:T(2,128)S(1)}, u32[]{:S(2)}, u32[]{:S(2)}) collective-permute-start(f32[5,2,2048]{2,1,0:T(2,128)S(1)} %get-tuple-element.63), channel_id=1, source_target_pairs={{1,0},{2,1},{3,2},{4,3},{5,4},{6,5},{7,6},{8,7},{9,8},{10,9},{11,1... | collective-permute-start | bytes 245768 | tf_op jit(solution)/shard_map/ppermute | solution.py:18
  12.5 0.8 copy-start.1
  15.3 0.7 copy-start.2
  16.8 6.6 %collective-permute-start.4 = (f32[5,2,2048]{2,1,0:T(2,128)S(1)}, f32[5,2,2048]{2,1,0:T(2,128)S(1)}, u32[]{:S(2)}, u32[]{:S(2)}) collective-permute-start(f32[5,2,2048]{2,1,0:T(2,128)S(1)} %get-tuple-element.54), channel_id=1, source_target_pairs={{0,1},{1,2},{2,3},{3,4},{4,5},{5,6},{6,7},{7,8},{8,9},{9,10},{10,1... | collective-permute-start | bytes 245768 | tf_op jit(solution)/shard_map/ppermute | solution.py:16
  16.8 6.6 %collective-permute-start.5 = (f32[5,2,2048]{2,1,0:T(2,128)S(1)}, f32[5,2,2048]{2,1,0:T(2,128)S(1)}, u32[]{:S(2)}, u32[]{:S(2)}) collective-permute-start(f32[5,2,2048]{2,1,0:T(2,128)S(1)} %get-tuple-element.53), channel_id=1, source_target_pairs={{1,0},{2,1},{3,2},{4,3},{5,4},{6,5},{7,6},{8,7},{9,8},{10,9},{11,1... | collective-permute-start | bytes 245768 | tf_op jit(solution)/shard_map/ppermute | solution.py:18
  25.3 6.6 %collective-permute-start.6 = (f32[5,2,2048]{2,1,0:T(2,128)S(1)}, f32[5,2,2048]{2,1,0:T(2,128)S(1)}, u32[]{:S(2)}, u32[]{:S(2)}) collective-permute-start(f32[5,2,2048]{2,1,0:T(2,128)S(1)} %get-tuple-element.44), channel_id=1, source_target_pairs={{0,1},{1,2},{2,3},{3,4},{4,5},{5,6},{6,7},{7,8},{8,9},{9,10},{10,1... | collective-permute-start | bytes 245768 | tf_op jit(solution)/shard_map/ppermute | solution.py:16
  25.3 6.6 %collective-permute-start.7 = (f32[5,2,2048]{2,1,0:T(2,128)S(1)}, f32[5,2,2048]{2,1,0:T(2,128)S(1)}, u32[]{:S(2)}, u32[]{:S(2)}) collective-permute-start(f32[5,2,2048]{2,1,0:T(2,128)S(1)} %get-tuple-element.43), channel_id=1, source_target_pairs={{1,0},{2,1},{3,2},{4,3},{5,4},{6,5},{7,6},{8,7},{9,8},{10,9},{11,1... | collective-permute-start | bytes 245768 | tf_op jit(solution)/shard_map/ppermute | solution.py:18
  32.9 0.7 copy-start.3
  33.3 9.3 %collective-permute-start.8 = (f32[5,8,2048]{2,1,0:T(8,128)S(1)}, f32[5,8,2048]{2,1,0:T(8,128)S(1)}, u32[]{:S(2)}, u32[]{:S(2)}) collective-permute-start(f32[5,8,2048]{2,1,0:T(8,128)S(1)} %fusion.66), channel_id=1, source_target_pairs={{0,1},{1,2},{2,3},{3,4},{4,5},{5,6},{6,7},{7,8},{8,9},{9,10},{10,1... | collective-permute-start | bytes 983048 | tf_op jit(solution)/shard_map/ppermute | solution.py:28
  42.7 10.4 %collective-permute-start.9 = (f32[5,8,2048]{2,1,0:T(8,128)S(1)}, f32[5,8,2048]{2,1,0:T(8,128)S(1)}, u32[]{:S(2)}, u32[]{:S(2)}) collective-permute-start(f32[5,8,2048]{2,1,0:T(8,128)S(1)} %broadcast_select_fusion), channel_id=1, source_target_pairs={{0,2},{1,3},{2,4},{3,5},{4,6},{5,7},{6,8},{7,9},{8,10},{9,11},{10,... | collective-permute-start | bytes 983048 | tf_op jit(solution)/shard_map/ppermute | solution.py:28
  53.1 11.8 %collective-permute-start.10 = (f32[5,8,2048]{2,1,0:T(8,128)S(1)}, f32[5,8,2048]{2,1,0:T(8,128)S(1)}, u32[]{:S(2)}, u32[]{:S(2)}) collective-permute-start(f32[5,8,2048]{2,1,0:T(8,128)S(1)} %broadcast_select_fusion.1), channel_id=1, source_target_pairs={{0,4},{1,5},{2,6},{3,7},{4,8},{5,9},{6,10},{7,11},{8,12},{9,13},{1... | collective-permute-start | bytes 983048 | tf_op jit(solution)/shard_map/ppermute | solution.py:28
  64.9 10.6 %collective-permute-start.11 = (f32[5,8,2048]{2,1,0:T(8,128)S(1)}, f32[5,8,2048]{2,1,0:T(8,128)S(1)}, u32[]{:S(2)}, u32[]{:S(2)}) collective-permute-start(f32[5,8,2048]{2,1,0:T(8,128)S(1)} %broadcast_select_fusion.2), channel_id=1, source_target_pairs={{0,8},{1,9},{2,10},{3,11},{4,12},{5,13},{6,14},{7,15},{8,0},{9,1},... | collective-permute-start | bytes 983048 | tf_op jit(solution)/shard_map/ppermute | solution.py:28
  75.6 9.2 %collective-permute-start.12 = (f32[5,8,2048]{2,1,0:T(8,128)S(1)}, f32[5,8,2048]{2,1,0:T(8,128)S(1)}, u32[]{:S(2)}, u32[]{:S(2)}) collective-permute-start(f32[5,8,2048]{2,1,0:T(8,128)S(1)} %broadcast_select_fusion.3), channel_id=1, source_target_pairs={{0,1},{1,2},{2,3},{3,4},{4,5},{5,6},{6,7},{7,8},{8,9},{9,10},{10,1... | collective-permute-start | bytes 983048 | tf_op jit(solution)/shard_map/ppermute | solution.py:28
  85.7 6.6 %collective-permute-start.13 = (f32[5,2,2048]{2,1,0:T(2,128)S(1)}, f32[5,2,2048]{2,1,0:T(2,128)S(1)}, u32[]{:S(2)}, u32[]{:S(2)}) collective-permute-start(f32[5,2,2048]{2,1,0:T(2,128)S(1)} %get-tuple-element.14), channel_id=1, source_target_pairs={{0,1},{1,2},{2,3},{3,4},{4,5},{5,6},{6,7},{7,8},{8,9},{9,10},{10,1... | collective-permute-start | bytes 245768 | tf_op jit(solution)/shard_map/ppermute | solution.py:16
  85.7 6.6 %collective-permute-start.14 = (f32[5,2,2048]{2,1,0:T(2,128)S(1)}, f32[5,2,2048]{2,1,0:T(2,128)S(1)}, u32[]{:S(2)}, u32[]{:S(2)}) collective-permute-start(f32[5,2,2048]{2,1,0:T(2,128)S(1)} %get-tuple-element.13), channel_id=1, source_target_pairs={{1,0},{2,1},{3,2},{4,3},{5,4},{6,5},{7,6},{8,7},{9,8},{10,9},{11,1... | collective-permute-start | bytes 245768 | tf_op jit(solution)/shard_map/ppermute | solution.py:18
  94.1 6.7 %collective-permute-start.15 = (f32[5,2,2048]{2,1,0:T(2,128)S(1)}, f32[5,2,2048]{2,1,0:T(2,128)S(1)}, u32[]{:S(2)}, u32[]{:S(2)}) collective-permute-start(f32[5,2,2048]{2,1,0:T(2,128)S(1)} %get-tuple-element.34), channel_id=1, source_target_pairs={{0,1},{1,2},{2,3},{3,4},{4,5},{5,6},{6,7},{7,8},{8,9},{9,10},{10,1... | collective-permute-start | bytes 245768 | tf_op jit(solution)/shard_map/ppermute | solution.py:16
  94.1 6.7 %collective-permute-start.16 = (f32[5,2,2048]{2,1,0:T(2,128)S(1)}, f32[5,2,2048]{2,1,0:T(2,128)S(1)}, u32[]{:S(2)}, u32[]{:S(2)}) collective-permute-start(f32[5,2,2048]{2,1,0:T(2,128)S(1)} %get-tuple-element.33), channel_id=1, source_target_pairs={{1,0},{2,1},{3,2},{4,3},{5,4},{6,5},{7,6},{8,7},{9,8},{10,9},{11,1... | collective-permute-start | bytes 245768 | tf_op jit(solution)/shard_map/ppermute | solution.py:18
  102.7 6.6 %collective-permute-start.17 = (f32[5,2,2048]{2,1,0:T(2,128)S(1)}, f32[5,2,2048]{2,1,0:T(2,128)S(1)}, u32[]{:S(2)}, u32[]{:S(2)}) collective-permute-start(f32[5,2,2048]{2,1,0:T(2,128)S(1)} %get-tuple-element.24), channel_id=1, source_target_pairs={{0,1},{1,2},{2,3},{3,4},{4,5},{5,6},{6,7},{7,8},{8,9},{9,10},{10,1... | collective-permute-start | bytes 245768 | tf_op jit(solution)/shard_map/ppermute | solution.py:16
  102.7 6.8 %collective-permute-start.18 = (f32[5,2,2048]{2,1,0:T(2,128)S(1)}, f32[5,2,2048]{2,1,0:T(2,128)S(1)}, u32[]{:S(2)}, u32[]{:S(2)}) collective-permute-start(f32[5,2,2048]{2,1,0:T(2,128)S(1)} %get-tuple-element.23), channel_id=1, source_target_pairs={{1,0},{2,1},{3,2},{4,3},{5,4},{6,5},{7,6},{8,7},{9,8},{10,9},{11,1... | collective-permute-start | bytes 245768 | tf_op jit(solution)/shard_map/ppermute | solution.py:18
  110.9 9.4 %collective-permute-start.19 = (f32[5,8,2048]{2,1,0:T(8,128)S(1)}, f32[5,8,2048]{2,1,0:T(8,128)S(1)}, u32[]{:S(2)}, u32[]{:S(2)}) collective-permute-start(f32[5,8,2048]{2,1,0:T(8,128)S(1)} %fusion.41), channel_id=1, source_target_pairs={{0,1},{1,2},{2,3},{3,4},{4,5},{5,6},{6,7},{7,8},{8,9},{9,10},{10,1... | collective-permute-start | bytes 983048 | tf_op jit(solution)/shard_map/ppermute | solution.py:28
  120.3 10.4 %collective-permute-start.20 = (f32[5,8,2048]{2,1,0:T(8,128)S(1)}, f32[5,8,2048]{2,1,0:T(8,128)S(1)}, u32[]{:S(2)}, u32[]{:S(2)}) collective-permute-start(f32[5,8,2048]{2,1,0:T(8,128)S(1)} %broadcast_select_fusion.4), channel_id=1, source_target_pairs={{0,2},{1,3},{2,4},{3,5},{4,6},{5,7},{6,8},{7,9},{8,10},{9,11},{10,... | collective-permute-start | bytes 983048 | tf_op jit(solution)/shard_map/ppermute | solution.py:28
  130.7 11.9 %collective-permute-start.21 = (f32[5,8,2048]{2,1,0:T(8,128)S(1)}, f32[5,8,2048]{2,1,0:T(8,128)S(1)}, u32[]{:S(2)}, u32[]{:S(2)}) collective-permute-start(f32[5,8,2048]{2,1,0:T(8,128)S(1)} %broadcast_select_fusion.5), channel_id=1, source_target_pairs={{0,4},{1,5},{2,6},{3,7},{4,8},{5,9},{6,10},{7,11},{8,12},{9,13},{1... | collective-permute-start | bytes 983048 | tf_op jit(solution)/shard_map/ppermute | solution.py:28
  142.6 10.5 %collective-permute-start.22 = (f32[5,8,2048]{2,1,0:T(8,128)S(1)}, f32[5,8,2048]{2,1,0:T(8,128)S(1)}, u32[]{:S(2)}, u32[]{:S(2)}) collective-permute-start(f32[5,8,2048]{2,1,0:T(8,128)S(1)} %broadcast_select_fusion.6), channel_id=1, source_target_pairs={{0,8},{1,9},{2,10},{3,11},{4,12},{5,13},{6,14},{7,15},{8,0},{9,1},... | collective-permute-start | bytes 983048 | tf_op jit(solution)/shard_map/ppermute | solution.py:28
  153.2 9.2 %collective-permute-start.23 = (f32[5,8,2048]{2,1,0:T(8,128)S(1)}, f32[5,8,2048]{2,1,0:T(8,128)S(1)}, u32[]{:S(2)}, u32[]{:S(2)}) collective-permute-start(f32[5,8,2048]{2,1,0:T(8,128)S(1)} %broadcast_select_fusion.7), channel_id=1, source_target_pairs={{0,1},{1,2},{2,3},{3,4},{4,5},{5,6},{6,7},{7,8},{8,9},{9,10},{10,1... | collective-permute-start | bytes 983048 | tf_op jit(solution)/shard_map/ppermute | solution.py:28
where the time goes:
time: 164 us; the launch traced here: 163 us
  waiting for transfers between devices  112 us (68%)
  starting transfers between devices  33.5 us (20%)
  other arithmetic  10.1 us (6%)
  local copies, waits for them, and re-layouts  6.99 us (4%)
    ppermute x10, waiting for transfers between devices, shifted(): return lax.ppermute(value, axis, pairs)  102 us
    ppermute x7, starting transfers between devices, padded(): lax.ppermute(head, axis, [((i + 1) % count, i) for i in range(count)])  32.3 us
    ppermute x7, waiting for transfers between devices, padded(): lax.ppermute(tail, axis, [(i, (i + 1) % count) for i in range(count)])  10.7 us
  transfers between devices with their start and end apart: 24, of which 17 were waited for; matrix products, arithmetic and copies ran while one was open for 1% of the time, Pallas kernels for 0%

commit v1 on v0

--- a/solution.py
+++ b/solution.py
@@ -1,9 +1,16 @@
+import functools
+
 import jax
 import jax.numpy as jnp
 from jax import lax
+from jax.experimental import pallas as pl
+from jax.experimental.pallas import tpu as pltpu
 from jax.sharding import PartitionSpec as P
 
 STEPS = 2
+HALO = 3
+LANES = 128
+SUBLANES = 8
 
 
 def padded(cells, sides, width):
@@ -76,7 +83,7 @@
     return current
 
 
-def local(conserved, velocity, viscosity, shifts):
+def by_azimuth(conserved, velocity, viscosity, shifts):
     state = conserved
     block = state.shape[1]
     heights = state.shape[2] // shifts.shape[1]
@@ -106,6 +113,311 @@
     return state
 
 
+def disc_kernel(
+    n,
+    heights,
+    cons,
+    vel,
+    visc,
+    shifts,
+    out,
+    ubuf,
+    u,
+    vp,
+    vn,
+    t1,
+    t2,
+    obuf,
+    a_send,
+    a_recv,
+    v_send,
+    v_recv,
+    h_send,
+    h_recv,
+    o_send,
+    o_recv,
+    own_sem,
+):
+    fields, block, cols = cons.shape
+    width = cols // n
+    owned = width // heights
+    azim = n * block
+    rim = HALO * heights
+    me = lax.axis_index("azim")
+
+    barrier = pltpu.get_barrier_semaphore()
+
+    def greet(k, carry):
+        pl.semaphore_signal(barrier, inc=1, device_id={"azim": lax.rem(me + k, n)})
+        return carry
+
+    lax.fori_loop(1, n, greet, 0)
+    pl.semaphore_wait(barrier, n - 1)
+
+    def lanes(d):
+        return pl.ds(pl.multiple_of(d * width, width), width)
+
+    def rows(d):
+        return pl.ds(pl.multiple_of(d * block, block), block)
+
+    def send_in(k):
+        to = lax.rem(me + k, n)
+        return (
+            pltpu.make_async_remote_copy(
+                src_ref=vel.at[:, lanes(to)],
+                dst_ref=ubuf.at[fields, rows(me), :],
+                send_sem=v_send.at[k],
+                recv_sem=v_recv.at[k],
+                device_id={"azim": to},
+            ),
+            pltpu.make_async_remote_copy(
+                src_ref=cons.at[:, :, lanes(to)],
+                dst_ref=ubuf.at[pl.ds(0, fields), rows(me), :],
+                send_sem=a_send.at[k],
+                recv_sem=a_recv.at[k],
+                device_id={"azim": to},
+            ),
+        )
+
+    def start_in(k, carry):
+        for copy in send_in(k):
+            copy.start()
+        return carry
+
+    lax.fori_loop(1, n, start_in, 0)
+    own_v = pltpu.make_async_copy(vel.at[:, lanes(me)], ubuf.at[fields, rows(me), :], own_sem.at[0])
+    own_u = pltpu.make_async_copy(
+        cons.at[:, :, lanes(me)], ubuf.at[pl.ds(0, fields), rows(me), :], own_sem.at[1]
+    )
+    own_v.start()
+    own_u.start()
+    own_v.wait()
+    own_u.wait()
+
+    def wait_in(k, carry):
+        source = lax.rem(me + n - k, n)
+        for copy in send_in(k):
+            copy.wait_send()
+        pltpu.make_async_remote_copy(
+            src_ref=vel.at[:, lanes(source)],
+            dst_ref=ubuf.at[fields, rows(source), :],
+            send_sem=v_send.at[k],
+            recv_sem=v_recv.at[k],
+            device_id={"azim": source},
+        ).wait_recv()
+        pltpu.make_async_remote_copy(
+            src_ref=cons.at[:, :, lanes(source)],
+            dst_ref=ubuf.at[pl.ds(0, fields), rows(source), :],
+            send_sem=a_send.at[k],
+            recv_sem=a_recv.at[k],
+            device_id={"azim": source},
+        ).wait_recv()
+        return carry
+
+    lax.fori_loop(1, n, wait_in, 0)
+
+    def turn(f, carry):
+        u[0, f, rim : rim + width, :] = ubuf[f].T
+        return carry
+
+    lax.fori_loop(0, fields + 1, turn, 0)
+
+    def halo(step, planes):
+        inner = pltpu.make_async_remote_copy(
+            src_ref=u.at[step, pl.ds(0, planes), pl.ds(rim, rim), :],
+            dst_ref=u.at[step, pl.ds(0, planes), pl.ds(rim + width, rim), :],
+            send_sem=h_send.at[step, 0],
+            recv_sem=h_recv.at[step, 0],
+            device_id={"azim": lax.rem(me + n - 1, n)},
+        )
+        outer = pltpu.make_async_remote_copy(
+            src_ref=u.at[step, pl.ds(0, planes), pl.ds(width, rim), :],
+            dst_ref=u.at[step, pl.ds(0, planes), pl.ds(0, rim), :],
+            send_sem=h_send.at[step, 1],
+            recv_sem=h_recv.at[step, 1],
+            device_id={"azim": lax.rem(me + 1, n)},
+        )
+
+        @pl.when(me > 0)
+        def _():
+            inner.start()
+
+        @pl.when(me < n - 1)
+        def _():
+            outer.start()
+
+        @pl.when(me > 0)
+        def _():
+            inner.wait_send()
+            outer.wait_recv()
+
+        @pl.when(me < n - 1)
+        def _():
+            outer.wait_send()
+            inner.wait_recv()
+
+    top = lax.broadcasted_iota(jnp.int32, (heights, azim), 0) == heights - 1
+    radii = owned + 2 * HALO
+
+    def part(r):
+        return slice(r * heights, (r + 1) * heights)
+
+    def stage(load, nu, first, last, write):
+        here = load(first)
+        below = here - load(first - 1)
+        if first == HALO:
+            below = jnp.where(me == 0, 0.0, below)
+        for r in range(first, last):
+            after = load(r + 1)
+            above = after - here
+            if r + 1 == HALO:
+                above = jnp.where(me == 0, 0.0, above)
+            if r + 1 == HALO + owned:
+                above = jnp.where(me == n - 1, 0.0, above)
+            x = here
+            d = x - pltpu.roll(x, 1, 1)
+            dp = pltpu.roll(d, azim - 1, 1)
+            low = jnp.minimum(d, dp)
+            high = jnp.maximum(d, dp)
+            half = 0.5 * (jnp.maximum(low, 0.0) + jnp.minimum(high, 0.0))
+            p = vp[part(r), :] * (x + half)
+            q = vn[part(r), :] * (x - half)
+            change = (p - q) + (pltpu.roll(q, azim - 1, 1) - pltpu.roll(p, 1, 1))
+            e = jnp.where(top, 0.0, pltpu.roll(x, heights - 1, 0) - x)
+            spread = (dp - d) + (e - pltpu.roll(e, 1, 0)) + (above - below)
+            write(r, x, nu * spread - change)
+            here = after
+            below = above
+
+    for step in range(STEPS):
+        halo(step, fields + 1 if step == 0 else fields)
+        if step == 0:
+            for r in range(1, radii - 1):
+                v = u[0, fields, part(r), :]
+                speed = 0.5 * (v + pltpu.roll(v, 1, 1))
+                vn[part(r), :] = jnp.minimum(speed, 0.0)
+                vp[part(r), :] = pltpu.roll(jnp.maximum(speed, 0.0), azim - 1, 1)
+
+        def advance(f, carry):
+            nu = visc[f]
+
+            def write1(r, x, change):
+                t1[part(r), :] = x + change
+
+            def write2(r, x, change):
+                t2[part(r), :] = 0.75 * u[step, f, part(r), :] + 0.25 * (x + change)
+
+            def write3(r, x, change):
+                y = (1.0 / 3.0) * u[step, f, part(r), :] + (2.0 / 3.0) * (x + change)
+                amount = shifts[step, me * owned + (r - HALO)]
+                y = pltpu.roll(y, amount, 1)
+                if step + 1 < STEPS:
+                    u[step + 1, f, part(r), :] = y
+                else:
+                    t1[part(r), :] = y
+
+            stage(lambda r: u[step, f, part(r), :], nu, 1, radii - 1, write1)
+            stage(lambda r: t1[part(r), :], nu, 2, radii - 2, write2)
+            stage(lambda r: t2[part(r), :], nu, 3, radii - 3, write3)
+            if step + 1 == STEPS:
+                obuf[f] = t1[rim : rim + width, :].T
+            return carry
+
+        lax.fori_loop(0, fields, advance, 0)
+
+    def send_out(k):
+        to = lax.rem(me + k, n)
+        return pltpu.make_async_remote_copy(
+            src_ref=obuf.at[:, rows(to), :],
+            dst_ref=out.at[:, :, lanes(me)],
+            send_sem=o_send.at[k],
+            recv_sem=o_recv.at[k],
+            device_id={"azim": to},
+        )
+
+    def start_out(k, carry):
+        send_out(k).start()
+        return carry
+
+    lax.fori_loop(1, n, start_out, 0)
+    own_o = pltpu.make_async_copy(obuf.at[:, rows(me), :], out.at[:, :, lanes(me)], own_sem.at[0])
+    own_o.start()
+    own_o.wait()
+
+    def wait_out(k, carry):
+        source = lax.rem(me + n - k, n)
+        send_out(k).wait_send()
+        pltpu.make_async_remote_copy(
+            src_ref=obuf.at[:, rows(source), :],
+            dst_ref=out.at[:, :, lanes(source)],
+            send_sem=o_send.at[k],
+            recv_sem=o_recv.at[k],
+            device_id={"azim": source},
+        ).wait_recv()
+        return carry
+
+    lax.fori_loop(1, n, wait_out, 0)
+
+
+def by_radius(conserved, velocity, viscosity, shifts):
+    fields, block, cols = conserved.shape
+    n = lax.axis_size("azim")
+    heights = cols // shifts.shape[1]
+    width = cols // n
+    wide = width + 2 * HALO * heights
+    azim = n * block
+    f32 = jnp.float32
+    dma = pltpu.SemaphoreType.DMA
+    return pl.pallas_call(
+        functools.partial(disc_kernel, n, heights),
+        out_shape=jax.ShapeDtypeStruct(conserved.shape, f32),
+        in_specs=[
+            pl.BlockSpec(memory_space=pl.ANY),
+            pl.BlockSpec(memory_space=pl.ANY),
+            pl.BlockSpec(memory_space=pltpu.SMEM),
+            pl.BlockSpec(memory_space=pltpu.SMEM),
+        ],
+        out_specs=pl.BlockSpec(memory_space=pl.ANY),
+        scratch_shapes=[
+            pltpu.VMEM((fields + 1, azim, width), f32),
+            pltpu.VMEM((STEPS, fields + 1, wide, azim), f32),
+            pltpu.VMEM((wide, azim), f32),
+            pltpu.VMEM((wide, azim), f32),
+            pltpu.VMEM((wide, azim), f32),
+            pltpu.VMEM((wide, azim), f32),
+            pltpu.VMEM((fields, azim, width), f32),
+            dma((n,)),
+            dma((n,)),
+            dma((n,)),
+            dma((n,)),
+            dma((STEPS, 2)),
+            dma((STEPS, 2)),
+            dma((n,)),
+            dma((n,)),
+            dma((2,)),
+        ],
+        compiler_params=pltpu.CompilerParams(collective_id=0, has_side_effects=True),
+    )(conserved, velocity, viscosity, shifts)
+
+
+def local(conserved, velocity, viscosity, shifts):
+    fields, block, cols = conserved.shape
+    n = lax.axis_size("azim")
+    heights = cols // shifts.shape[1]
+    fits = (
+        n * block == LANES
+        and cols % n == 0
+        and cols // n == LANES
+        and block % SUBLANES == 0
+        and heights % SUBLANES == 0
+        and LANES % heights == 0
+        and LANES // heights >= HALO
+    )
+    if fits:
+        return by_radius(conserved, velocity, viscosity, shifts)
+    return by_azimuth(conserved, velocity, viscosity, shifts)
+
+
 def solution(mesh):
     in_specs = (
         P(None, ("groups", "azim"), None),

time: 164 us -> 48.4 us (0.30)
  waiting for transfers between devices: 112 us -> 0 us
  Pallas kernels: 0 us -> 46.4 us
  starting transfers between devices: 33.5 us -> 0 us
  other arithmetic: 10.1 us -> 0 us
  local copies, waits for them, and re-layouts: 6.99 us -> 1.72 us
    ppermute x24 -> x0, waiting for transfers between devices: 112 us -> none  [the longest x10 102 us: shifted(): return lax.ppermute(value, axis, pairs)]
    pallas_call x0 -> x1, Pallas kernels: none -> 46.4 us  [by_radius(): pl.pallas_call(functools.partial(disc_kernel, n, heights), out_shape=jax....]
    ppermute x24 -> x0, starting transfers between devices: 33.5 us -> none  [the longest x7 32.3 us: padded(): lax.ppermute(head, axis, [((i + 1) % count, i) for i in range(count)])]
    slice x32 -> x0, local copies, waits for them, and re-layouts: 5.18 us -> none  [the longest x12 1.4 us: lateral_sum(): lower = jnp.concatenate([inner[:, :, :1], inner[:, :, :width - 1]], axis=2)]
    add x12 -> x0, other arithmetic: 4.44 us -> none  [the longest x6 1.77 us: tendency(): jnp.maximum(face_speed, 0.0) * left_state]
    mul x6 -> x0, other arithmetic: 2.82 us -> none  [minmod(): 0.5 * (jnp.sign(left) + jnp.sign(right))]
  transfers between devices with their start and end apart: 24 -> 0, of which waited for: 17 -> 0; matrix products, arithmetic and copies ran while one was open for 1% -> 0% of each run, Pallas kernels for 0% -> 0%
where the time goes in v1:
time: 48.4 us; the launch traced here: 48.2 us
  Pallas kernels  46.4 us (96%)
  local copies, waits for them, and re-layouts  1.72 us (4%)
    pallas_call x1, Pallas kernels, by_radius(): pl.pallas_call(functools.partial(disc_kernel, n, heights), out_shape=jax....  46.4 us
    unnamed x1, local copies, waits for them, and re-layouts  1.72 us

profile of v1, /device:TPU:0, one launch (start us, length us, event | category | flops | bytes accessed | tf_op | source)
XLA Modules:
  0.0 48.2 jit_solution(7438120425885151901)
XLA Ops:
  0.0 46.4 %shard_map.46 = f32[5,8,2048]{2,1,0:T(8,128)} custom-call(f32[5,8,2048]{2,1,0:T(8,128)} %cons.1, f32[8,2048]{1,0:T(8,128)} %vel.1, f32[5]{0:T(128)} %visc.1, s32[2,64]{1,0:T(2,128)} %shifts.1), custom_call_target="tpu_custom_call" | custom-call | tf_op jit(solution)/shard_map/pallas_call | solution.py:371
  46.4 1.7 %copy.6 = f32[5,8,2048]{2,1,0:T(8,128)} copy(f32[5,8,2048]{2,1,0:T(8,128)} %shard_map.46) | data formatting | bytes 655360

commit v2 on v0

--- a/solution.py
+++ b/solution.py
@@ -1,9 +1,16 @@
+import functools
+
 import jax
 import jax.numpy as jnp
 from jax import lax
+from jax.experimental import pallas as pl
+from jax.experimental.pallas import tpu as pltpu
 from jax.sharding import PartitionSpec as P
 
 STEPS = 2
+HALO = 3
+LANES = 128
+SUBLANES = 8
 
 
 def padded(cells, sides, width):
@@ -76,7 +83,7 @@
     return current
 
 
-def local(conserved, velocity, viscosity, shifts):
+def by_azimuth(conserved, velocity, viscosity, shifts):
     state = conserved
     block = state.shape[1]
     heights = state.shape[2] // shifts.shape[1]
@@ -106,6 +113,322 @@
     return state
 
 
+def winding(d):
+    row, chip, core = d // 4, (d % 4) // 2, d % 2
+    return row * 4 + ((row + chip) % 2) * 2 + core
+
+
+def disc_kernel(
+    n,
+    heights,
+    cons,
+    vel,
+    visc,
+    shifts,
+    out,
+    ubuf,
+    u,
+    vp,
+    vn,
+    t1,
+    t2,
+    obuf,
+    a_send,
+    a_recv,
+    a_own,
+    h_send,
+    h_recv,
+    o_send,
+    o_recv,
+    o_own,
+):
+    fields, block, cols = cons.shape
+    width = cols // n
+    owned = width // heights
+    azim = n * block
+    rim = HALO * heights
+    me = lax.axis_index("azim")
+    place = winding(me)
+    inward = winding(lax.rem(place + n - 1, n))
+    outward = winding(lax.rem(place + 1, n))
+
+    barrier = pltpu.get_barrier_semaphore()
+
+    def greet(k, carry):
+        pl.semaphore_signal(barrier, inc=1, device_id={"azim": lax.rem(me + k, n)})
+        return carry
+
+    lax.fori_loop(1, n, greet, 0)
+    pl.semaphore_wait(barrier, n - 1)
+
+    def lanes(d):
+        return pl.ds(pl.multiple_of(d * width, width), width)
+
+    def rows(d):
+        return pl.ds(pl.multiple_of(d * block, block), block)
+
+    def share(f, d):
+        return vel.at[:, lanes(winding(d))] if f is None else cons.at[f, :, lanes(winding(d))]
+
+    def send_in(f):
+        plane = fields if f is None else f
+
+        def one(k, carry):
+            to = lax.rem(me + k, n)
+            pltpu.make_async_remote_copy(
+                src_ref=share(f, to),
+                dst_ref=ubuf.at[plane, rows(me), :],
+                send_sem=a_send.at[plane],
+                recv_sem=a_recv.at[plane],
+                device_id={"azim": to},
+            ).start()
+            return carry
+
+        lax.fori_loop(1, n, one, 0)
+        pltpu.make_async_copy(share(f, me), ubuf.at[plane, rows(me), :], a_own.at[plane]).start()
+
+    def all_in(plane):
+        others = ubuf.at[plane, pl.ds(0, azim - block), :]
+        return pltpu.make_async_remote_copy(
+            src_ref=others,
+            dst_ref=others,
+            send_sem=a_send.at[plane],
+            recv_sem=a_recv.at[plane],
+            device_id={"azim": outward},
+        )
+
+    def halo(step, plane):
+        inner = pltpu.make_async_remote_copy(
+            src_ref=u.at[step, plane, pl.ds(rim, rim), :],
+            dst_ref=u.at[step, plane, pl.ds(rim + width, rim), :],
+            send_sem=h_send.at[step, 0, plane],
+            recv_sem=h_recv.at[step, 0, plane],
+            device_id={"azim": inward},
+        )
+        outer = pltpu.make_async_remote_copy(
+            src_ref=u.at[step, plane, pl.ds(width, rim), :],
+            dst_ref=u.at[step, plane, pl.ds(0, rim), :],
+            send_sem=h_send.at[step, 1, plane],
+            recv_sem=h_recv.at[step, 1, plane],
+            device_id={"azim": outward},
+        )
+        return inner, outer
+
+    def halo_start(step, plane):
+        inner, outer = halo(step, plane)
+        pl.when(place > 0)(inner.start)
+        pl.when(place < n - 1)(outer.start)
+
+    def halo_recv(step, plane):
+        inner, outer = halo(step, plane)
+        pl.when(place > 0)(outer.wait_recv)
+        pl.when(place < n - 1)(inner.wait_recv)
+
+    def halo_sent(step, plane):
+        inner, outer = halo(step, plane)
+        pl.when(place > 0)(inner.wait_send)
+        pl.when(place < n - 1)(outer.wait_send)
+
+    def arrive(plane):
+        pltpu.make_async_copy(
+            ubuf.at[plane, rows(me), :], ubuf.at[plane, rows(me), :], a_own.at[plane]
+        ).wait()
+        all_in(plane).wait_recv()
+        u[0, plane, rim : rim + width, :] = ubuf[plane].T
+        halo_start(0, plane)
+
+    def send_out(f):
+        def one(k, carry):
+            to = lax.rem(me + k, n)
+            pltpu.make_async_remote_copy(
+                src_ref=obuf.at[f, rows(to), :],
+                dst_ref=out.at[f, :, lanes(place)],
+                send_sem=o_send.at[f],
+                recv_sem=o_recv.at[f],
+                device_id={"azim": to},
+            ).start()
+            return carry
+
+        lax.fori_loop(1, n, one, 0)
+        pltpu.make_async_copy(obuf.at[f, rows(me), :], out.at[f, :, lanes(place)], o_own.at[f]).start()
+
+    top = lax.broadcasted_iota(jnp.int32, (heights, azim), 0) == heights - 1
+    radii = owned + 2 * HALO
+
+    def part(r):
+        return slice(r * heights, (r + 1) * heights)
+
+    def stage(load, nu, first, last, write):
+        here = load(first)
+        below = here - load(first - 1)
+        if first == HALO:
+            below = jnp.where(place == 0, 0.0, below)
+        for r in range(first, last):
+            after = load(r + 1)
+            above = after - here
+            if r + 1 == HALO:
+                above = jnp.where(place == 0, 0.0, above)
+            if r + 1 == HALO + owned:
+                above = jnp.where(place == n - 1, 0.0, above)
+            x = here
+            d = x - pltpu.roll(x, 1, 1)
+            dp = pltpu.roll(d, azim - 1, 1)
+            low = jnp.minimum(d, dp)
+            high = jnp.maximum(d, dp)
+            half = 0.5 * (jnp.maximum(low, 0.0) + jnp.minimum(high, 0.0))
+            p = vp[part(r), :] * (x + half)
+            q = vn[part(r), :] * (x - half)
+            change = (p - q) + (pltpu.roll(q, azim - 1, 1) - pltpu.roll(p, 1, 1))
+            e = jnp.where(top, 0.0, pltpu.roll(x, heights - 1, 0) - x)
+            spread = (dp - d) + (e - pltpu.roll(e, 1, 0)) + (above - below)
+            write(r, x, nu * spread - change)
+            here = after
+            below = above
+
+    def advance(step, f):
+        nu = visc[f]
+
+        def write1(r, x, change):
+            t1[part(r), :] = x + change
+
+        def write2(r, x, change):
+            t2[part(r), :] = 0.75 * u[step, f, part(r), :] + 0.25 * (x + change)
+
+        def write3(r, x, change):
+            y = (1.0 / 3.0) * u[step, f, part(r), :] + (2.0 / 3.0) * (x + change)
+            amount = shifts[step, place * owned + (r - HALO)]
+            y = pltpu.roll(y, amount, 1)
+            if step + 1 < STEPS:
+                u[step + 1, f, part(r), :] = y
+            else:
+                t1[part(r), :] = y
+
+        stage(lambda r: u[step, f, part(r), :], nu, 1, radii - 1, write1)
+        stage(lambda r: t1[part(r), :], nu, 2, radii - 2, write2)
+        stage(lambda r: t2[part(r), :], nu, 3, radii - 3, write3)
+
+    def each(body, count=fields):
+        def one(f, carry):
+            body(f)
+            return carry
+
+        lax.fori_loop(0, count, one, 0)
+
+    send_in(None)
+    each(send_in)
+    arrive(fields)
+    arrive(0)
+    halo_recv(0, fields)
+    for r in range(1, radii - 1):
+        v = u[0, fields, part(r), :]
+        speed = 0.5 * (v + pltpu.roll(v, 1, 1))
+        vn[part(r), :] = jnp.minimum(speed, 0.0)
+        vp[part(r), :] = pltpu.roll(jnp.maximum(speed, 0.0), azim - 1, 1)
+
+    for step in range(STEPS):
+
+        def work(f):
+            if step == 0:
+
+                @pl.when(f + 1 < fields)
+                def _():
+                    arrive(f + 1)
+
+            halo_recv(step, f)
+            advance(step, f)
+            if step + 1 < STEPS:
+                halo_start(step + 1, f)
+            else:
+                obuf[f] = t1[rim : rim + width, :].T
+                send_out(f)
+
+        each(work)
+
+    def sent(plane):
+        all_in(plane).wait_send()
+        halo_sent(0, plane)
+
+    each(sent, fields + 1)
+
+    def finish(f):
+        for step in range(1, STEPS):
+            halo_sent(step, f)
+        pltpu.make_async_copy(
+            obuf.at[f, rows(me), :], out.at[f, :, lanes(place)], o_own.at[f]
+        ).wait()
+        others = obuf.at[f, pl.ds(0, azim - block), :]
+        done = pltpu.make_async_remote_copy(
+            src_ref=others,
+            dst_ref=others,
+            send_sem=o_send.at[f],
+            recv_sem=o_recv.at[f],
+            device_id={"azim": outward},
+        )
+        done.wait_send()
+        done.wait_recv()
+
+    each(finish)
+
+
+def by_radius(conserved, velocity, viscosity, shifts):
+    fields, block, cols = conserved.shape
+    n = lax.axis_size("azim")
+    heights = cols // shifts.shape[1]
+    width = cols // n
+    wide = width + 2 * HALO * heights
+    azim = n * block
+    f32 = jnp.float32
+    dma = pltpu.SemaphoreType.DMA
+    return pl.pallas_call(
+        functools.partial(disc_kernel, n, heights),
+        out_shape=jax.ShapeDtypeStruct(conserved.shape, f32),
+        in_specs=[
+            pl.BlockSpec(memory_space=pl.ANY),
+            pl.BlockSpec(memory_space=pl.ANY),
+            pl.BlockSpec(memory_space=pltpu.SMEM),
+            pl.BlockSpec(memory_space=pltpu.SMEM),
+        ],
+        out_specs=pl.BlockSpec(memory_space=pl.ANY),
+        scratch_shapes=[
+            pltpu.VMEM((fields + 1, azim, width), f32),
+            pltpu.VMEM((STEPS, fields + 1, wide, azim), f32),
+            pltpu.VMEM((wide, azim), f32),
+            pltpu.VMEM((wide, azim), f32),
+            pltpu.VMEM((wide, azim), f32),
+            pltpu.VMEM((wide, azim), f32),
+            pltpu.VMEM((fields, azim, width), f32),
+            dma((fields + 1,)),
+            dma((fields + 1,)),
+            dma((fields + 1,)),
+            dma((STEPS, 2, fields + 1)),
+            dma((STEPS, 2, fields + 1)),
+            dma((fields,)),
+            dma((fields,)),
+            dma((fields,)),
+        ],
+        compiler_params=pltpu.CompilerParams(collective_id=0, has_side_effects=True),
+    )(conserved, velocity, viscosity, shifts)
+
+
+def local(conserved, velocity, viscosity, shifts):
+    fields, block, cols = conserved.shape
+    n = lax.axis_size("azim")
+    heights = cols // shifts.shape[1]
+    fits = (
+        n % 8 == 0
+        and n * block == LANES
+        and cols % n == 0
+        and cols // n == LANES
+        and block % SUBLANES == 0
+        and heights % SUBLANES == 0
+        and LANES % heights == 0
+        and LANES // heights >= HALO
+    )
+    if fits:
+        return by_radius(conserved, velocity, viscosity, shifts)
+    return by_azimuth(conserved, velocity, viscosity, shifts)
+
+
 def solution(mesh):
     in_specs = (
         P(None, ("groups", "azim"), None),

time: 164 us -> 39 us (0.24)
  waiting for transfers between devices: 112 us -> 0 us
  Pallas kernels: 0 us -> 37.1 us
  starting transfers between devices: 33.5 us -> 0 us
  other arithmetic: 10.1 us -> 0 us
  local copies, waits for them, and re-layouts: 6.99 us -> 1.72 us
    ppermute x24 -> x0, waiting for transfers between devices: 112 us -> none  [the longest x10 102 us: shifted(): return lax.ppermute(value, axis, pairs)]
    pallas_call x0 -> x1, Pallas kernels: none -> 37.1 us  [by_radius(): pl.pallas_call(functools.partial(disc_kernel, n, heights), out_shape=jax....]
    ppermute x24 -> x0, starting transfers between devices: 33.5 us -> none  [the longest x7 32.3 us: padded(): lax.ppermute(head, axis, [((i + 1) % count, i) for i in range(count)])]
    slice x32 -> x0, local copies, waits for them, and re-layouts: 5.18 us -> none  [the longest x12 1.4 us: lateral_sum(): lower = jnp.concatenate([inner[:, :, :1], inner[:, :, :width - 1]], axis=2)]
    add x12 -> x0, other arithmetic: 4.44 us -> none  [the longest x6 1.77 us: tendency(): jnp.maximum(face_speed, 0.0) * left_state]
    mul x6 -> x0, other arithmetic: 2.82 us -> none  [minmod(): 0.5 * (jnp.sign(left) + jnp.sign(right))]
  transfers between devices with their start and end apart: 24 -> 0, of which waited for: 17 -> 0; matrix products, arithmetic and copies ran while one was open for 1% -> 0% of each run, Pallas kernels for 0% -> 0%
where the time goes in v2:
time: 39 us; the launch traced here: 38.8 us
  Pallas kernels  37.1 us (95%)
  local copies, waits for them, and re-layouts  1.72 us (4%)
    pallas_call x1, Pallas kernels, by_radius(): pl.pallas_call(functools.partial(disc_kernel, n, heights), out_shape=jax....  37.1 us
    unnamed x1, local copies, waits for them, and re-layouts  1.72 us

profile of v2, /device:TPU:0, one launch (start us, length us, event | category | flops | bytes accessed | tf_op | source)
XLA Modules:
  0.0 38.8 jit_solution(15869325346948426943)
XLA Ops:
  0.0 37.1 %shard_map.46 = f32[5,8,2048]{2,1,0:T(8,128)} custom-call(f32[5,8,2048]{2,1,0:T(8,128)} %cons.1, f32[8,2048]{1,0:T(8,128)} %vel.1, f32[5]{0:T(128)} %visc.1, s32[2,64]{1,0:T(2,128)} %shifts.1), custom_call_target="tpu_custom_call" | custom-call | tf_op jit(solution)/shard_map/pallas_call | solution.py:382
  37.1 1.7 %copy.6 = f32[5,8,2048]{2,1,0:T(8,128)} copy(f32[5,8,2048]{2,1,0:T(8,128)} %shard_map.46) | data formatting | bytes 655360

commit v3 on v2

--- a/solution.py
+++ b/solution.py
@@ -123,9 +123,12 @@
     heights,
     cons,
     vel,
+    visc_in,
+    shifts_in,
+    out,
     visc,
     shifts,
-    out,
+    s_own,
     ubuf,
     u,
     vp,
@@ -141,6 +144,10 @@
     o_send,
     o_recv,
     o_own,
+    xbuf,
+    x_send,
+    x_recv,
+    x_own,
 ):
     fields, block, cols = cons.shape
     width = cols // n
@@ -151,6 +158,7 @@
     place = winding(me)
     inward = winding(lax.rem(place + n - 1, n))
     outward = winding(lax.rem(place + 1, n))
+    middle = n // 2
 
     barrier = pltpu.get_barrier_semaphore()
 
@@ -186,6 +194,45 @@
 
         lax.fori_loop(1, n, one, 0)
         pltpu.make_async_copy(share(f, me), ubuf.at[plane, rows(me), :], a_own.at[plane]).start()
+        for taker, giver in ((middle - 1, middle), (middle, middle - 1)):
+
+            @pl.when(place != taker)
+            def _():
+                pltpu.make_async_remote_copy(
+                    src_ref=share(f, winding(giver)),
+                    dst_ref=xbuf.at[plane, rows(me), :],
+                    send_sem=x_send.at[plane],
+                    recv_sem=x_recv.at[plane],
+                    device_id={"azim": winding(taker)},
+                ).start()
+
+            @pl.when(place == taker)
+            def _():
+                pltpu.make_async_copy(
+                    share(f, winding(giver)), xbuf.at[plane, rows(me), :], x_own.at[plane]
+                ).start()
+
+    def cross(plane, count):
+        others = xbuf.at[plane, pl.ds(0, count * block), :]
+        return pltpu.make_async_remote_copy(
+            src_ref=others,
+            dst_ref=others,
+            send_sem=x_send.at[plane],
+            recv_sem=x_recv.at[plane],
+            device_id={"azim": outward},
+        )
+
+    def cross_in(plane):
+        pltpu.make_async_copy(
+            xbuf.at[plane, rows(me), :], xbuf.at[plane, rows(me), :], x_own.at[plane]
+        ).wait()
+        cross(plane, n - 1).wait_recv()
+        return xbuf[plane].T
+
+    def linked(step):
+        if step == 0:
+            return (place > 0) & (place != middle), (place < n - 1) & (place != middle - 1)
+        return place > 0, place < n - 1
 
     def all_in(plane):
         others = ubuf.at[plane, pl.ds(0, azim - block), :]
@@ -216,18 +263,21 @@
 
     def halo_start(step, plane):
         inner, outer = halo(step, plane)
-        pl.when(place > 0)(inner.start)
-        pl.when(place < n - 1)(outer.start)
+        back, ahead = linked(step)
+        pl.when(back)(inner.start)
+        pl.when(ahead)(outer.start)
 
     def halo_recv(step, plane):
         inner, outer = halo(step, plane)
-        pl.when(place > 0)(outer.wait_recv)
-        pl.when(place < n - 1)(inner.wait_recv)
+        back, ahead = linked(step)
+        pl.when(back)(outer.wait_recv)
+        pl.when(ahead)(inner.wait_recv)
 
     def halo_sent(step, plane):
         inner, outer = halo(step, plane)
-        pl.when(place > 0)(inner.wait_send)
-        pl.when(place < n - 1)(outer.wait_send)
+        back, ahead = linked(step)
+        pl.when(back)(inner.wait_send)
+        pl.when(ahead)(outer.wait_send)
 
     def arrive(plane):
         pltpu.make_async_copy(
@@ -236,6 +286,14 @@
         all_in(plane).wait_recv()
         u[0, plane, rim : rim + width, :] = ubuf[plane].T
         halo_start(0, plane)
+
+        @pl.when(place == middle - 1)
+        def _():
+            u[0, plane, rim + width : rim + width + rim, :] = cross_in(plane)[:rim]
+
+        @pl.when(place == middle)
+        def _():
+            u[0, plane, 0:rim, :] = cross_in(plane)[width - rim :]
 
     def send_out(f):
         def one(k, carry):
@@ -314,10 +372,18 @@
 
         lax.fori_loop(0, count, one, 0)
 
+    scalars = (
+        pltpu.make_async_copy(visc_in, visc, s_own.at[0]),
+        pltpu.make_async_copy(shifts_in, shifts, s_own.at[1]),
+    )
+    for copy in scalars:
+        copy.start()
     send_in(None)
     each(send_in)
     arrive(fields)
     arrive(0)
+    for copy in scalars:
+        copy.wait()
     halo_recv(0, fields)
     for r in range(1, radii - 1):
         v = u[0, fields, part(r), :]
@@ -346,6 +412,9 @@
 
     def sent(plane):
         all_in(plane).wait_send()
+        at_middle = (place == middle - 1) | (place == middle)
+        pl.when(at_middle)(cross(plane, 1).wait_send)
+        pl.when(jnp.logical_not(at_middle))(cross(plane, 2).wait_send)
         halo_sent(0, plane)
 
     each(sent, fields + 1)
@@ -385,11 +454,14 @@
         in_specs=[
             pl.BlockSpec(memory_space=pl.ANY),
             pl.BlockSpec(memory_space=pl.ANY),
-            pl.BlockSpec(memory_space=pltpu.SMEM),
-            pl.BlockSpec(memory_space=pltpu.SMEM),
+            pl.BlockSpec(memory_space=pl.ANY),
+            pl.BlockSpec(memory_space=pl.ANY),
         ],
         out_specs=pl.BlockSpec(memory_space=pl.ANY),
         scratch_shapes=[
+            pltpu.SMEM(viscosity.shape, f32),
+            pltpu.SMEM(shifts.shape, jnp.int32),
+            dma((2,)),
             pltpu.VMEM((fields + 1, azim, width), f32),
             pltpu.VMEM((STEPS, fields + 1, wide, azim), f32),
             pltpu.VMEM((wide, azim), f32),
@@ -405,6 +477,10 @@
             dma((fields,)),
             dma((fields,)),
             dma((fields,)),
+            pltpu.VMEM((fields + 1, azim, width), f32),
+            dma((fields + 1,)),
+            dma((fields + 1,)),
+            dma((fields + 1,)),
         ],
         compiler_params=pltpu.CompilerParams(collective_id=0, has_side_effects=True),
     )(conserved, velocity, viscosity, shifts)

time: 39 us -> 37.6 us (0.964)
  Pallas kernels: 37.1 us -> 35.8 us
    pallas_call x1, Pallas kernels: 37.1 us -> 35.8 us  [by_radius(): pl.pallas_call(functools.partial(disc_kernel, n, heights), out_shape=jax....]
where the time goes in v3:
time: 37.6 us; the launch traced here: 37.5 us
  Pallas kernels  35.8 us (95%)
  local copies, waits for them, and re-layouts  1.72 us (5%)
    pallas_call x1, Pallas kernels, by_radius(): pl.pallas_call(functools.partial(disc_kernel, n, heights), out_shape=jax....  35.8 us
    unnamed x1, local copies, waits for them, and re-layouts  1.72 us

profile of v3, /device:TPU:0, one launch (start us, length us, event | category | flops | bytes accessed | tf_op | source)
XLA Modules:
  0.0 37.5 jit_solution(17568365082649109593)
XLA Ops:
  0.0 35.8 %shard_map.46 = f32[5,8,2048]{2,1,0:T(8,128)} custom-call(f32[5,8,2048]{2,1,0:T(8,128)} %cons.1, f32[8,2048]{1,0:T(8,128)} %vel.1, f32[5]{0:T(128)} %visc_in.1, s32[2,64]{1,0:T(2,128)} %shifts_in.1), custom_call_target="tpu_custom_call" | custom-call | tf_op jit(solution)/shard_map/pallas_call | solution.py:451
  35.8 1.7 %copy.6 = f32[5,8,2048]{2,1,0:T(8,128)} copy(f32[5,8,2048]{2,1,0:T(8,128)} %shard_map.46) | data formatting | bytes 655360

commit v4 on v3

--- a/solution.py
+++ b/solution.py
@@ -382,6 +382,7 @@
     each(send_in)
     arrive(fields)
     arrive(0)
+    arrive(1)
     for copy in scalars:
         copy.wait()
     halo_recv(0, fields)
@@ -396,9 +397,9 @@
         def work(f):
             if step == 0:
 
-                @pl.when(f + 1 < fields)
+                @pl.when(f + 2 < fields)
                 def _():
-                    arrive(f + 1)
+                    arrive(f + 2)
 
             halo_recv(step, f)
             advance(step, f)

time: 37.6 us -> 35.8 us (0.952)
  Pallas kernels: 35.8 us -> 34 us
    pallas_call x1, Pallas kernels: 35.8 us -> 34 us  [by_radius(): pl.pallas_call(functools.partial(disc_kernel, n, heights), out_shape=jax....]
where the time goes in v4:
time: 35.8 us; the launch traced here: 35.7 us
  Pallas kernels  34 us (95%)
  local copies, waits for them, and re-layouts  1.72 us (5%)
    pallas_call x1, Pallas kernels, by_radius(): pl.pallas_call(functools.partial(disc_kernel, n, heights), out_shape=jax....  34 us
    unnamed x1, local copies, waits for them, and re-layouts  1.72 us

profile of v4, /device:TPU:0, one launch (start us, length us, event | category | flops | bytes accessed | tf_op | source)
XLA Modules:
  0.0 35.7 jit_solution(7226489186110586845)
XLA Ops:
  0.0 34.0 %shard_map.46 = f32[5,8,2048]{2,1,0:T(8,128)} custom-call(f32[5,8,2048]{2,1,0:T(8,128)} %cons.1, f32[8,2048]{1,0:T(8,128)} %vel.1, f32[5]{0:T(128)} %visc_in.1, s32[2,64]{1,0:T(2,128)} %shifts_in.1), custom_call_target="tpu_custom_call" | custom-call | tf_op jit(solution)/shard_map/pallas_call | solution.py:452
  34.0 1.7 %copy.6 = f32[5,8,2048]{2,1,0:T(8,128)} copy(f32[5,8,2048]{2,1,0:T(8,128)} %shard_map.46) | data formatting | bytes 655360
